TPU v7x, 32 devices: a whole 2x2x4 slice. The times are simulated.
32 devices in a mesh: gz: 4 (over y, x), gy: 2 (over core), gx: 4 (over z).
Axes of the slice: x: 2, y: 2, z: 4, core: 2. Of those that a mesh axis runs over, the one named last changes fastest.
Arguments:
- populations: float32 [19, 32, 16, 512], P(None, 'gz', 'gy', 'gx'), may hold values from 0.1 to 20, as said below
- solid: int32 [32, 16, 512], P('gz', 'gy', 'gx'), may hold values 0 or 1
- ports: int32 [2, 16, 512], P(None, 'gy', 'gx'), may hold values 0 or 1
- concentration: float32 [2, 4, 2, 64], P(None, 'gz'), may hold values from 0 to 1
- loaded: float32 [2, 4, 2, 64], P(None, 'gz'), may hold values from 0 to 2
Outputs:
- final_populations: float32 [19, 32, 16, 512], P(None, 'gz', 'gy', 'gx')
- new_concentration: float32 [2, 4, 2, 64], P(None, 'gz')
- new_loaded: float32 [2, 4, 2, 64], P(None, 'gz')
Inputs may be any that keep to these rules, and one draw needn't show every extreme that they name: `populations`: every population is positive and of the size of its lattice weight times 36.
All inputs are finite; a program needn't handle non-finite values. No bound on the sum of `solid` or of `ports` on one device may be relied on, other than what follows from the above.
Results may differ from a plain program's by a relative error of at most 0.00002.
Values sent between devices are 32-bit elements; how exact they have to be, the bound alone decides.
A program may use at most 64 MiB of HBM per device.

v0:
```python
import jax
import jax.numpy as jnp
from jax import lax
from jax.sharding import PartitionSpec as P

ITERS = 2
lattice = [
    (0, 0, 0),
    (1, 0, 0),
    (-1, 0, 0),
    (0, 1, 0),
    (0, -1, 0),
    (0, 0, 1),
    (0, 0, -1),
    (1, 1, 0),
    (-1, -1, 0),
    (1, -1, 0),
    (-1, 1, 0),
    (1, 0, 1),
    (-1, 0, -1),
    (1, 0, -1),
    (-1, 0, 1),
    (0, 1, 1),
    (0, -1, -1),
    (0, 1, -1),
    (0, -1, 1),
]
opposite = [0, 2, 1, 4, 3, 6, 5, 8, 7, 10, 9, 12, 11, 14, 13, 16, 15, 18, 17]
weights = [1.0 / 3.0] + [1.0 / 18.0] * 6 + [1.0 / 36.0] * 12
relax_rate = 1.25
base_density = 36.0
inlet_speed = 0.05
spread_base = (0.03, 0.06)
spread_length = 0.1
uptake_rate = (0.3, 0.6)
affinity = (2.0, 0.5)
phase_ratio = 0.5
feed_level = (1.0, 0.5)


def extended(cells, sides, width, closed):
    for axis, dim in sides:
        count = lax.axis_size(axis)
        ends = count if closed else count - 1
        head = lax.slice_in_dim(cells, 0, width, axis=dim)
        tail = lax.slice_in_dim(cells, cells.shape[dim] - width, cells.shape[dim], axis=dim)
        cells = jnp.concatenate(
            [
                lax.ppermute(tail, axis, [(i, (i + 1) % count) for i in range(ends)]),
                cells,
                lax.ppermute(head, axis, [((i + 1) % count, i) for i in range(ends)]),
            ],
            axis=dim,
        )
    return cells


def equilibrium(density, velocity):
    speed_z, speed_y, speed_x = velocity
    square = speed_z * speed_z + speed_y * speed_y + speed_x * speed_x
    result = []
    for member in range(19):
        step_z, step_y, step_x = lattice[member]
        along = step_z * speed_z + step_y * speed_y + step_x * speed_x
        result.append(
            weights[member] * density * (1.0 + 3.0 * along + 4.5 * along * along - 1.5 * square)
        )
    return result


def moments(pops):
    density = pops[0]
    for member in range(1, 19):
        density = density + pops[member]
    flows = []
    for position in range(3):
        total = jnp.zeros_like(pops[0])
        for member in range(19):
            heading = lattice[member][position]
            if heading == 1:
                total = total + pops[member]
            elif heading == -1:
                total = total - pops[member]
        flows.append(total)
    return (density, flows)


def collide(pops, solid_flag):
    density, flows = moments(pops)
    velocity = [flow / density for flow in flows]
    balance = equilibrium(density, velocity)
    post = [
        jnp.where(
            solid_flag,
            pops[opposite[member]],
            pops[member] - relax_rate * (pops[member] - balance[member]),
        )
        for member in range(19)
    ]
    return (post, velocity)


def close_ends(moved, post, velocity, ports, first_dev, last_dev):
    inflow = equilibrium(base_density, (inlet_speed, 0.0, 0.0))
    outflow = equilibrium(base_density, (velocity[0][-1], velocity[1][-1], velocity[2][-1]))
    inlet_open = ports[0] == 1
    outlet_open = ports[1] == 1
    result = list(moved)
    for member in range(19):
        step_z = lattice[member][0]
        back = post[opposite[member]]
        if step_z == 1:
            entering = jnp.where(inlet_open, inflow[member], back[0])
            result[member] = (
                result[member].at[0].set(jnp.where(first_dev, entering, result[member][0]))
            )
        elif step_z == -1:
            entering = jnp.where(outlet_open, outflow[member], back[-1])
            result[member] = (
                result[member].at[-1].set(jnp.where(last_dev, entering, result[member][-1]))
            )
    return result


def block_sum(field):
    depth, height, width = field.shape
    return field.reshape(depth // 8, 8, height // 8, 8, width // 8, 8).sum(axis=(1, 3, 5))


def transport(padded, loaded, coarse_vel):
    centre = padded[:, 1:-1]
    neighbours = [
        (padded[:, :-2], padded[:, 2:]),
        (jnp.roll(centre, 1, axis=2), jnp.roll(centre, -1, axis=2)),
        (jnp.roll(centre, 1, axis=3), jnp.roll(centre, -1, axis=3)),
    ]
    change = jnp.zeros_like(centre)
    curvature = jnp.zeros_like(centre)
    reach = jnp.zeros_like(coarse_vel[0])
    for direction in range(3):
        courant = 8.0 * coarse_vel[direction]
        before, after = neighbours[direction]
        change = (
            change
            - jnp.maximum(courant, 0.0) * (centre - before)
            - jnp.minimum(courant, 0.0) * (after - centre)
        )
        curvature = curvature + after - 2.0 * centre + before
        reach = reach + jnp.abs(courant)
    base = jnp.array(spread_base, dtype=centre.dtype)[:, None, None, None]
    speed = jnp.array(uptake_rate, dtype=centre.dtype)[:, None, None, None]
    holding = jnp.array(affinity, dtype=centre.dtype)[:, None, None, None]
    rate = speed * (holding * centre - loaded)
    new_conc = centre + change + (base + spread_length * reach) * curvature - phase_ratio * rate
    return (new_conc, loaded + rate)


def body(populations, solid, ports, concentration, loaded):
    depth, height, width = solid.shape
    slab_pos = lax.axis_index("gz")
    first_dev = slab_pos == 0
    last_dev = slab_pos == lax.axis_size("gz") - 1
    pops = [populations[member] for member in range(19)]
    solid_flag = solid == 1
    for iteration in range(ITERS):
        post, velocity = collide(pops, solid_flag)
        padded = extended(jnp.stack(post), (("gz", 1), ("gy", 2), ("gx", 3)), 1, True)
        moved = []
        for member in range(19):
            step_z, step_y, step_x = lattice[member]
            moved.append(
                padded[
                    member,
                    1 - step_z : 1 - step_z + depth,
                    1 - step_y : 1 - step_y + height,
                    1 - step_x : 1 - step_x + width,
                ]
            )
        pops = close_ends(moved, post, velocity, ports, first_dev, last_dev)
    final = jnp.stack(pops)
    density, flows = moments(pops)
    fluid = (solid == 0).astype(jnp.float32)
    local = jnp.stack([block_sum(flow * fluid) for flow in flows]) / (512.0 * base_density)
    across = lax.all_gather(local, "gy", axis=2, tiled=True)
    coarse_vel = lax.all_gather(across, "gx", axis=3, tiled=True)
    padded_conc = extended(concentration, (("gz", 1),), 1, False)
    feed = jnp.broadcast_to(
        jnp.array(feed_level, dtype=jnp.float32)[:, None, None],
        (2, concentration.shape[2], concentration.shape[3]),
    )
    front = jnp.where(first_dev, feed, padded_conc[:, 0])
    rear = jnp.where(last_dev, concentration[:, -1], padded_conc[:, -1])
    padded_conc = padded_conc.at[:, 0].set(front).at[:, -1].set(rear)
    new_conc, new_load = transport(padded_conc, loaded, coarse_vel)
    return (final, new_conc, new_load)


def solution(mesh):
    placed = (
        P(None, "gz", "gy", "gx"),
        P("gz", "gy", "gx"),
        P(None, "gy", "gx"),
        P(None, "gz", None, None),
        P(None, "gz", None, None),
    )
    return jax.shard_map(
        body,
        mesh=mesh,
        in_specs=placed,
        out_specs=(P(None, "gz", "gy", "gx"), P(None, "gz", None, None), P(None, "gz", None, None)),
        check_vma=False,
    )
```

profile of v0, /device:TPU:0, one launch (start us, length us, event | category | flops | bytes accessed | tf_op | source)
XLA Modules:
  0.0 104.6 jit_solution(4216951791328130897)
XLA Ops:
  0.6 5.6 %collective-permute-start.12 = (f32[2,1,2,64]{3,2,1,0:T(2,128)}, f32[2,1,2,64]{3,2,1,0:T(2,128)}, u32[]{:S(2)}, u32[]{:S(2)}) collective-permute-start(f32[2,1,2,64]{3,2,1,0:T(2,128)} %param.56), channel_id=1, source_target_pairs={{0,8},{8,16},{16,24},{1,9},{9,17},{17,25},{2,10},{10,18},{18,26},{... | collective-permute-start | bytes 3080 | tf_op jit(solution)/shard_map/ppermute | solution.py:49
  6.2 1.3 %collective-permute-start.13 = (f32[2,1,2,64]{3,2,1,0:T(2,128)}, f32[2,1,2,64]{3,2,1,0:T(2,128)}, u32[]{:S(2)}, u32[]{:S(2)}) collective-permute-start(f32[2,1,2,64]{3,2,1,0:T(2,128)} %param.56), channel_id=1, source_target_pairs={{8,0},{16,8},{24,16},{9,1},{17,9},{25,17},{10,2},{18,10},{26,18},{... | collective-permute-start | bytes 3080 | tf_op jit(solution)/shard_map/ppermute | solution.py:51
  7.5 1.2 %constant_dynamic-update-slice_fusion.18 = (f32[19,8,8,128]{3,2,1,0:T(8,128)S(1)}, f32[8,8,128]{2,1,0:T(8,128)S(1)}, f32[8,8,128]{2,1,0:T(8,128)S(1)}, f32[8,8,1...) fusion(f32[19,8,8,128]{3,2,1,0:T(8,128)} %param.53, ...), kind=kLoop, calls=%fused_computation.20 | loop fusion | flops 589823 | bytes 860160
  8.7 0.8 constant_dynamic-update-slice_fusion.17
  9.5 0.8 constant_dynamic-update-slice_fusion.16
  10.3 0.8 constant_dynamic-update-slice_fusion.15
  11.8 2.7 %collective-permute-start = (f32[19,1,8,128]{3,2,1,0:T(8,128)S(1)}, f32[19,1,8,128]{3,2,1,0:T(8,128)S(1)}, u32[]{:S(2)}, u32[]{:S(2)}) collective-permute-start(f32[19,1,8,128]{3,2,1,0:T(8,128)S(1)} %get-tuple-element.383), channel_id=1, source_target_pairs={{0,8},{8,16},{16,24},{24,0},{1,9},{9,17},{17,25},{25,1},{2,10},{10... | collective-permute-start | bytes 233480 | tf_op jit(solution)/shard_map/ppermute | solution.py:49
  14.5 1.0 collective-permute-start.1
  15.6 0.7 fusion.359
  16.2 2.4 %collective-permute-done = f32[19,1,8,128]{3,2,1,0:T(8,128)S(1)} collective-permute-done((f32[19,1,8,128]{3,2,1,0:T(8,128)S(1)}, f32[19,1,8,128]{3,2,1,0:T(8,128)S(1)}, u32[]{:S(2)}, u32[]{:S(2)}) %collective-permute-start) | collective-permute-done | bytes 77856 | tf_op jit(solution)/shard_map/ppermute | solution.py:49
  18.6 0.9 collective-permute-done.1
  20.3 0.7 fusion.391
  21.5 1.7 %fusion.386 = (f32[19,10,10,1]{3,2,1,0:T(8,128)}, f32[19,10,10,1]{3,2,1,0:T(8,128)S(1)}) fusion(f32[19,10,10,128]{3,2,1,0:T(8,128)S(1)} %pad_maximum_fusion), kind=kLoop, calls=%fused_computation.679 | loop fusion | bytes 30400 | tf_op jit(solution)/shard_map/slice | solution.py:45
  23.2 2.1 %copy.55 = f32[19,10,10,1]{0,3,2,1:T(1,128)S(1)} copy(f32[19,10,10,1]{3,2,1,0:T(8,128)} %get-tuple-element.355) | data formatting | bytes 15200 | tf_op jit(solution)/shard_map/slice | solution.py:45
  25.4 3.6 %collective-permute-start.5 = (f32[19,10,10,1]{0,3,2,1:T(1,128)S(1)}, f32[19,10,10,1]{0,3,2,1:T(1,128)S(1)}, u32[]{:S(2)}, u32[]{:S(2)}) collective-permute-start(f32[19,10,10,1]{0,3,2,1:T(1,128)S(1)} %copy.55), channel_id=1, source_target_pairs={{1,0},{2,1},{3,2},{0,3},{5,4},{6,5},{7,6},{4,7},{9,8},{10,9},{11,1... | collective-permute-start | bytes 22808 | tf_op jit(solution)/shard_map/ppermute | solution.py:51
  29.0 0.8 copy.53
  29.9 1.1 %collective-permute-done.5 = f32[19,10,10,1]{0,3,2,1:T(1,128)S(1)} collective-permute-done((f32[19,10,10,1]{0,3,2,1:T(1,128)S(1)}, f32[19,10,10,1]{0,3,2,1:T(1,128)S(1)}, u32[]{:S(2)}, u32[]{:S(2)}) %collective-permute-start.5) | collective-permute-done | bytes 7632 | tf_op jit(solution)/shard_map/ppermute | solution.py:51
  31.0 1.6 %copy.56 = f32[19,10,10,1]{3,2,1,0:T(8,128)S(1)} copy(f32[19,10,10,1]{0,3,2,1:T(1,128)S(1)} %collective-permute-done.5) | data formatting | bytes 15200 | tf_op jit(solution)/shard_map/ppermute | solution.py:51
  32.7 3.0 %collective-permute-done.4 = f32[19,10,10,1]{0,3,2,1:T(1,128)S(1)} collective-permute-done((f32[19,10,10,1]{0,3,2,1:T(1,128)S(1)}, f32[19,10,10,1]{0,3,2,1:T(1,128)S(1)}, u32[]{:S(2)}, u32[]{:S(2)}) %collective-permute-start.4) | collective-permute-done | bytes 7632 | tf_op jit(solution)/shard_map/ppermute | solution.py:49
  35.7 2.7 %copy.54 = f32[19,10,10,1]{3,2,1,0:T(8,128)} copy(f32[19,10,10,1]{0,3,2,1:T(1,128)S(1)} %collective-permute-done.4) | data formatting | bytes 15200 | tf_op jit(solution)/shard_map/ppermute | solution.py:49
  38.4 1.0 maximum_bitcast_fusion.13
  39.5 1.3 %copy-done = f32[19,10,10,1]{3,2,1,0:T(8,128)S(1)} copy-done((f32[19,10,10,1]{3,2,1,0:T(8,128)S(1)}, f32[19,10,10,1]{3,2,1,0:T(8,128)}, u32[]{:S(2)}) %copy-start) | copy-done | bytes 7624
  41.8 0.7 constant_dynamic-update-slice_fusion.36
  42.4 0.6 constant_dynamic-update-slice_fusion.35
  43.2 0.6 constant_dynamic-update-slice_fusion.30
  43.9 0.6 constant_dynamic-update-slice_fusion.29
  44.5 0.6 constant_dynamic-update-slice_fusion.28
  45.1 0.6 constant_dynamic-update-slice_fusion.27
  45.8 0.6 constant_dynamic-update-slice_fusion.26
  46.4 0.6 constant_dynamic-update-slice_fusion.25
  47.0 0.6 constant_dynamic-update-slice_fusion.24
  47.7 0.6 constant_dynamic-update-slice_fusion.23
  48.5 2.1 %collective-permute-start.6 = (f32[19,1,8,128]{3,2,1,0:T(8,128)S(1)}, f32[19,1,8,128]{3,2,1,0:T(8,128)S(1)}, u32[]{:S(2)}, u32[]{:S(2)}) collective-permute-start(f32[19,1,8,128]{3,2,1,0:T(8,128)S(1)} %get-tuple-element.382), channel_id=1, source_target_pairs={{0,8},{8,16},{16,24},{24,0},{1,9},{9,17},{17,25},{25,1},{2,10},{10... | collective-permute-start | bytes 233480 | tf_op jit(solution)/shard_map/ppermute | solution.py:49
  50.6 0.8 collective-permute-start.7
  51.5 0.7 fusion.392
  52.1 1.7 %collective-permute-done.6 = f32[19,1,8,128]{3,2,1,0:T(8,128)S(1)} collective-permute-done((f32[19,1,8,128]{3,2,1,0:T(8,128)S(1)}, f32[19,1,8,128]{3,2,1,0:T(8,128)S(1)}, u32[]{:S(2)}, u32[]{:S(2)}) %collective-permute-start.6) | collective-permute-done | bytes 77856 | tf_op jit(solution)/shard_map/ppermute | solution.py:49
  53.8 1.2 %collective-permute-done.7 = f32[19,1,8,128]{3,2,1,0:T(8,128)S(1)} collective-permute-done((f32[19,1,8,128]{3,2,1,0:T(8,128)S(1)}, f32[19,1,8,128]{3,2,1,0:T(8,128)S(1)}, u32[]{:S(2)}, u32[]{:S(2)}) %collective-permute-start.7) | collective-permute-done | bytes 77856 | tf_op jit(solution)/shard_map/ppermute | solution.py:51
  55.7 0.6 fusion.390
  57.0 1.7 %fusion.385 = (f32[19,10,10,1]{3,2,1,0:T(8,128)S(1)}, f32[19,10,10,1]{3,2,1,0:T(8,128)}) fusion(f32[19,10,10,128]{3,2,1,0:T(8,128)S(1)} %pad_maximum_fusion.1), kind=kLoop, calls=%fused_computation.678 | loop fusion | bytes 30400 | tf_op jit(solution)/shard_map/slice | solution.py:45
  58.7 2.1 %copy.57 = f32[19,10,10,1]{0,3,2,1:T(1,128)S(1)} copy(f32[19,10,10,1]{3,2,1,0:T(8,128)} %get-tuple-element.354) | data formatting | bytes 15200 | tf_op jit(solution)/shard_map/slice | solution.py:46
  60.9 0.8 copy.59
  61.6 4.0 %collective-permute-start.11 = (f32[19,10,10,1]{0,3,2,1:T(1,128)S(1)}, f32[19,10,10,1]{0,3,2,1:T(1,128)}, u32[]{:S(2)}, u32[]{:S(2)}) collective-permute-start(f32[19,10,10,1]{0,3,2,1:T(1,128)S(1)} %copy.59), channel_id=1, source_target_pairs={{1,0},{2,1},{3,2},{0,3},{5,4},{6,5},{7,6},{4,7},{9,8},{10,9},{11,1... | collective-permute-start | bytes 22808 | tf_op jit(solution)/shard_map/ppermute | solution.py:51
  65.7 1.7 %collective-permute-done.11 = f32[19,10,10,1]{0,3,2,1:T(1,128)} collective-permute-done((f32[19,10,10,1]{0,3,2,1:T(1,128)S(1)}, f32[19,10,10,1]{0,3,2,1:T(1,128)}, u32[]{:S(2)}, u32[]{:S(2)}) %collective-permute-start.11) | collective-permute-done | bytes 7632 | tf_op jit(solution)/shard_map/ppermute | solution.py:51
  67.4 2.4 %copy.60 = f32[19,10,10,1]{3,2,1,0:T(8,128)S(1)} copy(f32[19,10,10,1]{0,3,2,1:T(1,128)} %collective-permute-done.11) | data formatting | bytes 15200 | tf_op jit(solution)/shard_map/ppermute | solution.py:51
  70.0 0.5 copy-done.13
  70.5 0.7 constant_dynamic-update-slice_fusion.64
  71.3 0.6 copy-done.4
  71.8 3.4 %copy.58 = f32[19,10,10,1]{3,2,1,0:T(8,128)} copy(f32[19,10,10,1]{0,3,2,1:T(1,128)} %collective-permute-done.10) | data formatting | bytes 15200 | tf_op jit(solution)/shard_map/ppermute | solution.py:49
  75.3 1.1 %maximum_bitcast_fusion.3 = (f32[8,8,128]{2,1,0:T(8,128)S(1)}, f32[8,8,128]{2,1,0:T(8,128)S(1)}, f32[8,8,128]{2,1,0:T(8,128)S(1)}) fusion(f32[19,10,10,1]{3,2,1,0:T(8,128)} %copy.58, f32[19,10,1,128]{3,2,1,0:T(1,128)S(1)} %collective-permute-done.9, f32[19,10,1,128]{3,2,1,0:T(1,128)S(1)} %collective-permute-done.8, ...), kind=kLoop, calls=%fused_computation.399 | loop fusion | flops 106496 | bytes 1078704 | tf_op jit(solution)/shard_map/squeeze | solution.py:172
  76.7 0.8 constant_dynamic-update-slice_fusion.57
  77.5 0.7 constant_dynamic-update-slice_fusion.61
  78.2 0.7 constant_dynamic-update-slice_fusion.59
  78.9 0.8 constant_dynamic-update-slice_fusion.60
  79.7 0.7 constant_dynamic-update-slice_fusion.63
  80.5 1.4 %select_reduce_fusion = (f32[128]{0:T(128)}, f32[128]{0:T(128)S(1)}, f32[128]{0:T(128)}, f32[1,8,8,128]{3,2,1,0:T(8,128)S(1)}, f32[1,8,8,128]{3,2,1,0:T(8,128)S(...) fusion(f32[8,8,128]{2,1,0:T(8,128)S(1)} %get-tuple-element.278,, ...), kind=kLoop, calls=%fused_computation.509 | loop fusion | flops 573056 | bytes 1612128 | tf_op jit(solution)/shard_map/reduce_sum | solution.py:127
  81.9 0.7 reduce_sum.37
  82.7 0.7 reduce_sum.40
  83.9 1.8 %all_gather.6 = f32[3,1,2,16]{3,1,0,2:T(1,128)S(1)} all-gather(f32[3,1,1,16]{3,1,0,2:T(1,128)S(1)} %fusion.358), channel_id=1, replica_groups=mesh['gz'=4,'gy'=2,'gx'=4] {'gy'}, dimensions={2}, use_global_device_ids=true | all-gather | bytes 576 | tf_op jit(solution)/shard_map/all_gather | solution.py:184
  85.8 13.6 %all_gather.7 = f32[3,1,2,64]{0,2,1,3:T(2,128)S(1)} all-gather(f32[3,1,2,16]{0,2,1,3:T(2,128)S(1)} %copy.62), channel_id=1, replica_groups=mesh['gz'=4,'gy'=2,'gx'=4] {'gx'}, dimensions={3}, use_global_device_ids=true | all-gather | bytes 1920 | tf_op jit(solution)/shard_map/all_gather | solution.py:185
  99.9 0.8 constant_dynamic-update-slice_fusion.53
  100.7 0.8 constant_dynamic-update-slice_fusion.52
  101.4 0.8 constant_dynamic-update-slice_fusion.51
  102.2 0.8 constant_dynamic-update-slice_fusion.50
  103.3 1.4 %multiply_subtract_fusion = f32[2,1,2,64]{3,2,1,0:T(2,128)} fusion(f32[2,1,2,64]{3,2,1,0:T(2,128)S(1)} %copy-done.9, f32[2,1,2,1]{3,2,1,0:T(2,128)S(1)} %copy-done.19, f32[2,1,2,63]{3,2,1,0:T(2,128)S(1)} %copy-done.21, f32[2,1,2,63]{3,2,1,0:T(2,128)S(1)} %copy-done.20, f32[2,1,2,1]{3,2,1,0:T(2,128)S(1)} %copy-done.18, f32[2,1,1,64]{3,2,1,0:T(1,128)S(1)} %copy-done.23, ...), kind=kLoop, calls=%fused_computation.666 | loop fusion | flops 10496 | bytes 11810 | tf_op jit(solution)/shard_map/sub | solution.py:154
  (138 shorter events, 6.6 us)
Async XLA Ops:
  0.6 10.5 %copy-start.2 = (f32[19,8,8,128]{3,2,1,0:T(8,128)S(1)}, f32[19,8,8,128]{3,2,1,0:T(8,128)}, u32[]{:S(2)}) copy-start(f32[19,8,8,128]{3,2,1,0:T(8,128)} %param.53) | copy-start | bytes 1867780
  0.6 102.5 %collective-permute-start.12 = (f32[2,1,2,64]{3,2,1,0:T(2,128)}, f32[2,1,2,64]{3,2,1,0:T(2,128)}, u32[]{:S(2)}, u32[]{:S(2)}) collective-permute-start(f32[2,1,2,64]{3,2,1,0:T(2,128)} %param.56), channel_id=1, source_target_pairs={{0,8},{8,16},{16,24},{1,9},{9,17},{17,25},{2,10},{10,18},{18,26},{... | collective-permute-start | bytes 3080 | tf_op jit(solution)/shard_map/ppermute | solution.py:49
  6.2 96.9 %collective-permute-start.13 = (f32[2,1,2,64]{3,2,1,0:T(2,128)}, f32[2,1,2,64]{3,2,1,0:T(2,128)}, u32[]{:S(2)}, u32[]{:S(2)}) collective-permute-start(f32[2,1,2,64]{3,2,1,0:T(2,128)} %param.56), channel_id=1, source_target_pairs={{8,0},{16,8},{24,16},{9,1},{17,9},{25,17},{10,2},{18,10},{26,18},{... | collective-permute-start | bytes 3080 | tf_op jit(solution)/shard_map/ppermute | solution.py:51
  11.3 4.3 %copy-start.8 = (f32[2,1,2,64]{3,2,1,0:T(2,128)S(1)}, f32[2,1,2,64]{3,2,1,0:T(2,128)}, u32[]{:S(2)}) copy-start(f32[2,1,2,64]{3,2,1,0:T(2,128)} %param.56) | copy-start | bytes 3076
  11.3 4.2 %copy-start.16 = (f32[2,1,2,64]{3,2,1,0:T(2,128)S(1)}, f32[2,1,2,64]{3,2,1,0:T(2,128)}, u32[]{:S(2)}) copy-start(f32[2,1,2,64]{3,2,1,0:T(2,128)} %param.57) | copy-start | bytes 3076
  11.3 4.2 %copy-start.24 = (f32[2]{0:T(128)S(1)}, f32[2]{0:T(128)}, u32[]{:S(2)}) copy-start(f32[2]{0:T(128)} %constant.557.clone) | copy-start | bytes 28
  11.3 4.2 %copy-start.26 = (f32[2]{0:T(128)S(1)}, f32[2]{0:T(128)}, u32[]{:S(2)}) copy-start(f32[2]{0:T(128)} %constant.558.clone) | copy-start | bytes 28
  11.8 6.8 %collective-permute-start = (f32[19,1,8,128]{3,2,1,0:T(8,128)S(1)}, f32[19,1,8,128]{3,2,1,0:T(8,128)S(1)}, u32[]{:S(2)}, u32[]{:S(2)}) collective-permute-start(f32[19,1,8,128]{3,2,1,0:T(8,128)S(1)} %get-tuple-element.383), channel_id=1, source_target_pairs={{0,8},{8,16},{16,24},{24,0},{1,9},{9,17},{17,25},{25,1},{2,10},{10... | collective-permute-start | bytes 233480 | tf_op jit(solution)/shard_map/ppermute | solution.py:49
  14.5 5.0 %collective-permute-start.1 = (f32[19,1,8,128]{3,2,1,0:T(8,128)S(1)}, f32[19,1,8,128]{3,2,1,0:T(8,128)S(1)}, u32[]{:S(2)}, u32[]{:S(2)}) collective-permute-start(f32[19,1,8,128]{3,2,1,0:T(8,128)S(1)} %get-tuple-element.384), channel_id=1, source_target_pairs={{8,0},{16,8},{24,16},{0,24},{9,1},{17,9},{25,17},{1,25},{10,2},{18... | collective-permute-start | bytes 233480 | tf_op jit(solution)/shard_map/ppermute | solution.py:51
  19.7 1.4 %collective-permute-start.2 = (f32[19,10,1,128]{3,2,1,0:T(1,128)S(1)}, f32[19,10,1,128]{3,2,1,0:T(1,128)S(1)}, u32[]{:S(2)}, u32[]{:S(2)}) collective-permute-start(f32[19,10,1,128]{3,2,1,0:T(1,128)S(1)} %get-tuple-element.375), channel_id=1, source_target_pairs={{0,4},{4,0},{1,5},{5,1},{2,6},{6,2},{3,7},{7,3},{8,12},{12,8},{9,1... | collective-permute-start | bytes 291848 | tf_op jit(solution)/shard_map/ppermute | solution.py:49
  19.8 1.4 %collective-permute-start.3 = (f32[19,10,1,128]{3,2,1,0:T(1,128)S(1)}, f32[19,10,1,128]{3,2,1,0:T(1,128)S(1)}, u32[]{:S(2)}, u32[]{:S(2)}) collective-permute-start(f32[19,10,1,128]{3,2,1,0:T(1,128)S(1)} %get-tuple-element.376), channel_id=1, source_target_pairs={{4,0},{0,4},{5,1},{1,5},{6,2},{2,6},{7,3},{3,7},{12,8},{8,12},{13,... | collective-permute-start | bytes 291848 | tf_op jit(solution)/shard_map/ppermute | solution.py:51
  25.4 4.5 %copy-start.15 = (s32[2,8,128]{2,1,0:T(8,128)S(1)}, s32[2,8,128]{2,1,0:T(8,128)}, u32[]{:S(2)}) copy-start(s32[2,8,128]{2,1,0:T(8,128)} %param.55) | copy-start | bytes 24580
  25.4 5.6 %collective-permute-start.5 = (f32[19,10,10,1]{0,3,2,1:T(1,128)S(1)}, f32[19,10,10,1]{0,3,2,1:T(1,128)S(1)}, u32[]{:S(2)}, u32[]{:S(2)}) collective-permute-start(f32[19,10,10,1]{0,3,2,1:T(1,128)S(1)} %copy.55), channel_id=1, source_target_pairs={{1,0},{2,1},{3,2},{0,3},{5,4},{6,5},{7,6},{4,7},{9,8},{10,9},{11,1... | collective-permute-start | bytes 22808 | tf_op jit(solution)/shard_map/ppermute | solution.py:51
  29.8 5.9 %collective-permute-start.4 = (f32[19,10,10,1]{0,3,2,1:T(1,128)S(1)}, f32[19,10,10,1]{0,3,2,1:T(1,128)S(1)}, u32[]{:S(2)}, u32[]{:S(2)}) collective-permute-start(f32[19,10,10,1]{0,3,2,1:T(1,128)S(1)} %copy.53), channel_id=1, source_target_pairs={{0,1},{1,2},{2,3},{3,0},{4,5},{5,6},{6,7},{7,4},{8,9},{9,10},{10,1... | collective-permute-start | bytes 22808 | tf_op jit(solution)/shard_map/ppermute | solution.py:49
  29.9 11.0 %copy-start.10 = (pred[1,8,128]{2,1,0:T(8,128)(4,1)}, pred[1,8,128]{2,1,0:T(8,128)(4,1)S(1)}, u32[]{:S(2)}) copy-start(pred[1,8,128]{2,1,0:T(8,128)(4,1)S(1)} %get-tuple-element.317) | copy-start | bytes 3076
  39.4 1.4 %copy-start = (f32[19,10,10,1]{3,2,1,0:T(8,128)S(1)}, f32[19,10,10,1]{3,2,1,0:T(8,128)}, u32[]{:S(2)}) copy-start(f32[19,10,10,1]{3,2,1,0:T(8,128)} %copy.54) | copy-start | bytes 22804
  40.9 0.6 copy-start.12
  48.5 5.3 %collective-permute-start.6 = (f32[19,1,8,128]{3,2,1,0:T(8,128)S(1)}, f32[19,1,8,128]{3,2,1,0:T(8,128)S(1)}, u32[]{:S(2)}, u32[]{:S(2)}) collective-permute-start(f32[19,1,8,128]{3,2,1,0:T(8,128)S(1)} %get-tuple-element.382), channel_id=1, source_target_pairs={{0,8},{8,16},{16,24},{24,0},{1,9},{9,17},{17,25},{25,1},{2,10},{10... | collective-permute-start | bytes 233480 | tf_op jit(solution)/shard_map/ppermute | solution.py:49
  50.6 4.4 %collective-permute-start.7 = (f32[19,1,8,128]{3,2,1,0:T(8,128)S(1)}, f32[19,1,8,128]{3,2,1,0:T(8,128)S(1)}, u32[]{:S(2)}, u32[]{:S(2)}) collective-permute-start(f32[19,1,8,128]{3,2,1,0:T(8,128)S(1)} %get-tuple-element.381), channel_id=1, source_target_pairs={{8,0},{16,8},{24,16},{0,24},{9,1},{17,9},{25,17},{1,25},{10,2},{18... | collective-permute-start | bytes 233480 | tf_op jit(solution)/shard_map/ppermute | solution.py:51
  55.2 1.4 %collective-permute-start.8 = (f32[19,10,1,128]{3,2,1,0:T(1,128)S(1)}, f32[19,10,1,128]{3,2,1,0:T(1,128)S(1)}, u32[]{:S(2)}, u32[]{:S(2)}) collective-permute-start(f32[19,10,1,128]{3,2,1,0:T(1,128)S(1)} %get-tuple-element.371), channel_id=1, source_target_pairs={{0,4},{4,0},{1,5},{5,1},{2,6},{6,2},{3,7},{7,3},{8,12},{12,8},{9,1... | collective-permute-start | bytes 291848 | tf_op jit(solution)/shard_map/ppermute | solution.py:49
  55.2 1.4 %collective-permute-start.9 = (f32[19,10,1,128]{3,2,1,0:T(1,128)S(1)}, f32[19,10,1,128]{3,2,1,0:T(1,128)S(1)}, u32[]{:S(2)}, u32[]{:S(2)}) collective-permute-start(f32[19,10,1,128]{3,2,1,0:T(1,128)S(1)} %get-tuple-element.372), channel_id=1, source_target_pairs={{4,0},{0,4},{5,1},{1,5},{6,2},{2,6},{7,3},{3,7},{12,8},{8,12},{13,... | collective-permute-start | bytes 291848 | tf_op jit(solution)/shard_map/ppermute | solution.py:51
  60.8 10.4 %collective-permute-start.10 = (f32[19,10,10,1]{0,3,2,1:T(1,128)S(1)}, f32[19,10,10,1]{0,3,2,1:T(1,128)}, u32[]{:S(2)}, u32[]{:S(2)}) collective-permute-start(f32[19,10,10,1]{0,3,2,1:T(1,128)S(1)} %copy.57), channel_id=1, source_target_pairs={{0,1},{1,2},{2,3},{3,0},{4,5},{5,6},{6,7},{7,4},{8,9},{9,10},{10,1... | collective-permute-start | bytes 22808 | tf_op jit(solution)/shard_map/ppermute | solution.py:49
  61.6 5.8 %collective-permute-start.11 = (f32[19,10,10,1]{0,3,2,1:T(1,128)S(1)}, f32[19,10,10,1]{0,3,2,1:T(1,128)}, u32[]{:S(2)}, u32[]{:S(2)}) collective-permute-start(f32[19,10,10,1]{0,3,2,1:T(1,128)S(1)} %copy.59), channel_id=1, source_target_pairs={{1,0},{2,1},{3,2},{0,3},{5,4},{6,5},{7,6},{4,7},{9,8},{10,9},{11,1... | collective-permute-start | bytes 22808 | tf_op jit(solution)/shard_map/ppermute | solution.py:51
  69.8 0.7 copy-start.13
  71.2 0.6 copy-start.4
  75.3 1.5 %copy-start.1 = (f32[19,10,10,1]{3,2,1,0:T(8,128)S(1)}, f32[19,10,10,1]{3,2,1,0:T(8,128)}, u32[]{:S(2)}) copy-start(f32[19,10,10,1]{3,2,1,0:T(8,128)} %copy.58) | copy-start | bytes 22804
  75.3 1.5 %copy-start.11 = (pred[1,8,128]{2,1,0:T(8,128)(4,1)S(1)}, pred[1,8,128]{2,1,0:T(8,128)(4,1)}, u32[]{:S(2)}) copy-start(pred[1,8,128]{2,1,0:T(8,128)(4,1)} %copy-done.10) | copy-start | bytes 3076
  77.5 1.4 %copy-start.14 = (pred[1,8,128]{2,1,0:T(8,128)(4,1)S(1)}, pred[1,8,128]{2,1,0:T(8,128)(4,1)}, u32[]{:S(2)}) copy-start(pred[1,8,128]{2,1,0:T(8,128)(4,1)} %copy-done.12) | copy-start | bytes 3076
  78.9 1.5 %copy-start.5 = (f32[8,8,128]{2,1,0:T(8,128)S(1)}, f32[8,8,128]{2,1,0:T(8,128)}, u32[]{:S(2)}) copy-start(f32[8,8,128]{2,1,0:T(8,128)} %copy-done.4) | copy-start | bytes 98308
  78.9 1.5 %copy-start.7 = (s32[8,8,128]{2,1,0:T(8,128)S(1)}, s32[8,8,128]{2,1,0:T(8,128)}, u32[]{:S(2)}) copy-start(s32[8,8,128]{2,1,0:T(8,128)} %param.54) | copy-start | bytes 98308
  81.8 21.2 %copy-start.6 = (f32[1,8,8,128]{3,2,1,0:T(8,128)S(1)}, f32[1,8,8,128]{3,2,1,0:T(8,128)}, u32[]{:S(2)}) copy-start(f32[1,8,8,128]{3,2,1,0:T(8,128)} %get-tuple-element.273) | copy-start | bytes 98308
  81.8 21.3 %copy-start.9 = (f32[2,1,2,64]{3,2,1,0:T(2,128)S(1)}, f32[2,1,2,64]{3,2,1,0:T(2,128)}, u32[]{:S(2)}) copy-start(f32[2,1,2,64]{3,2,1,0:T(2,128)} %param.56) | copy-start | bytes 3076
  81.8 21.3 %copy-start.17 = (f32[2,1,2,64]{3,2,1,0:T(2,128)S(1)}, f32[2,1,2,64]{3,2,1,0:T(2,128)}, u32[]{:S(2)}) copy-start(f32[2,1,2,64]{3,2,1,0:T(2,128)} %param.57) | copy-start | bytes 3076
  81.8 21.3 %copy-start.18 = (f32[2,1,2,1]{3,2,1,0:T(2,128)S(1)}, f32[2,1,2,1]{3,2,1,0:T(2,128)}, u32[]{:S(2)}) copy-start(f32[2,1,2,1]{3,2,1,0:T(2,128)} %get-tuple-element.394) | copy-start | bytes 52
  81.8 21.3 %copy-start.19 = (f32[2,1,2,1]{3,2,1,0:T(2,128)S(1)}, f32[2,1,2,1]{3,2,1,0:T(2,128)}, u32[]{:S(2)}) copy-start(f32[2,1,2,1]{3,2,1,0:T(2,128)} %get-tuple-element.395) | copy-start | bytes 52
  81.9 21.3 %copy-start.20 = (f32[2,1,2,63]{3,2,1,0:T(2,128)S(1)}, f32[2,1,2,63]{3,2,1,0:T(2,128)}, u32[]{:S(2)}) copy-start(f32[2,1,2,63]{3,2,1,0:T(2,128)} %get-tuple-element.396) | copy-start | bytes 3028
  81.9 21.3 %copy-start.21 = (f32[2,1,2,63]{3,2,1,0:T(2,128)S(1)}, f32[2,1,2,63]{3,2,1,0:T(2,128)}, u32[]{:S(2)}) copy-start(f32[2,1,2,63]{3,2,1,0:T(2,128)} %get-tuple-element.397) | copy-start | bytes 3028
  81.9 21.3 %copy-start.22 = (f32[2,1,1,64]{3,2,1,0:T(1,128)S(1)}, f32[2,1,1,64]{3,2,1,0:T(1,128)}, u32[]{:S(2)}) copy-start(f32[2,1,1,64]{3,2,1,0:T(1,128)} %get-tuple-element.392) | copy-start | bytes 1540
  81.9 21.3 %copy-start.23 = (f32[2,1,1,64]{3,2,1,0:T(1,128)S(1)}, f32[2,1,1,64]{3,2,1,0:T(1,128)}, u32[]{:S(2)}) copy-start(f32[2,1,1,64]{3,2,1,0:T(1,128)} %get-tuple-element.393) | copy-start | bytes 1540
  81.9 21.3 %copy-start.25 = (f32[2]{0:T(128)S(1)}, f32[2]{0:T(128)}, u32[]{:S(2)}) copy-start(f32[2]{0:T(128)} %constant.557.clone) | copy-start | bytes 28
  81.9 21.3 %copy-start.27 = (f32[2]{0:T(128)S(1)}, f32[2]{0:T(128)}, u32[]{:S(2)}) copy-start(f32[2]{0:T(128)} %constant.558.clone) | copy-start | bytes 28
  81.9 21.3 %copy-start.28 = (f32[2]{0:T(128)S(1)}, f32[2]{0:T(128)}, u32[]{:S(2)}) copy-start(f32[2]{0:T(128)} %constant.555.clone) | copy-start | bytes 28
  81.9 21.3 %copy-start.29 = (f32[2]{0:T(128)S(1)}, f32[2]{0:T(128)}, u32[]{:S(2)}) copy-start(f32[2]{0:T(128)} %constant.556.clone) | copy-start | bytes 28
  103.1 1.5 %copy-start.3 = (f32[19,8,8,128]{3,2,1,0:T(8,128)}, f32[19,8,8,128]{3,2,1,0:T(8,128)S(1)}, u32[]{:S(2)}) copy-start(f32[19,8,8,128]{3,2,1,0:T(8,128)S(1)} %constant_dynamic-update-slice_fusion.38) | copy-start | bytes 1867780
where the time goes:
time: 106 us; the launch traced here: 105 us
  local copies, waits for them, and re-layouts  29.9 us (28%)
  other arithmetic  22.8 us (22%)
  starting transfers between devices  22.4 us (21%)
  blocking collectives  15.5 us (15%)
  waiting for transfers between devices  12.7 us (12%)
  between operations  1.35 us (1%)
    all_gather x1, blocking collectives, body(): coarse_vel = lax.all_gather(across, 'gx', axis=3, tiled=True)  13.6 us
    ppermute x7, starting transfers between devices, extended(): lax.ppermute(head, axis, [((i + 1) % count, i) for i in range(ends)])  11.8 us
    unnamed x35, other arithmetic  10.8 us
    ppermute x7, starting transfers between devices, extended(): lax.ppermute(tail, axis, [(i, (i + 1) % count) for i in range(ends)])  10.6 us
    ppermute x7, waiting for transfers between devices, extended(): lax.ppermute(tail, axis, [(i, (i + 1) % count) for i in range(ends)])  7.47 us
    unnamed x82, local copies, waits for them, and re-layouts  6.83 us
    slice x5, local copies, waits for them, and re-layouts, extended(): head = lax.slice_in_dim(cells, 0, width, axis=dim)  6.35 us
    ppermute x2, local copies, waits for them, and re-layouts, extended(): lax.ppermute(tail, axis, [(i, (i + 1) % count) for i in range(ends)])  6.09 us
  transfers between devices with their start and end apart: 14, of which 11 were waited for; matrix products, arithmetic and copies ran while one was open for 46% of the time, Pallas kernels for 0%

commit v1 on v0

--- a/solution.py
+++ b/solution.py
@@ -38,6 +38,29 @@
 feed_level = (1.0, 0.5)
 
 
+def in_order(blocks, dim):
+    shape = list(blocks.shape[1:])
+    shape[dim] *= blocks.shape[0]
+    return jnp.moveaxis(blocks, 0, dim).reshape(shape)
+
+
+def doubled(x, axis):
+    devices, here = (lax.axis_size(axis), lax.axis_index(axis))
+    pieces, distance = (x[None], 1)
+    while distance < devices:
+        received = lax.ppermute(pieces, axis, [(i, i ^ distance) for i in range(devices)])
+        low = here & distance == 0
+        pieces = jnp.concatenate(
+            [jnp.where(low, pieces, received), jnp.where(low, received, pieces)]
+        )
+        distance *= 2
+    return pieces
+
+
+def gather_by_bits(value, axis, dim):
+    return in_order(doubled(value, axis), dim)
+
+
 def extended(cells, sides, width, closed):
     for axis, dim in sides:
         count = lax.axis_size(axis)
@@ -182,7 +205,7 @@
     fluid = (solid == 0).astype(jnp.float32)
     local = jnp.stack([block_sum(flow * fluid) for flow in flows]) / (512.0 * base_density)
     across = lax.all_gather(local, "gy", axis=2, tiled=True)
-    coarse_vel = lax.all_gather(across, "gx", axis=3, tiled=True)
+    coarse_vel = gather_by_bits(across, "gx", 3)
     padded_conc = extended(concentration, (("gz", 1),), 1, False)
     feed = jnp.broadcast_to(
         jnp.array(feed_level, dtype=jnp.float32)[:, None, None],

time: 106 us -> 100 us (0.943)
  blocking collectives: 15.5 us -> 1.83 us
  starting transfers between devices: 22.4 us -> 27.4 us
  waiting for transfers between devices: 12.7 us -> 14.3 us
  local copies, waits for them, and re-layouts: 29.9 us -> 31.3 us
    all_gather x1 -> x0, blocking collectives: 13.6 us -> none  [body(): coarse_vel = lax.all_gather(across, 'gx', axis=3, tiled=True)]
    ppermute x0 -> x2, starting transfers between devices: none -> 4.93 us  [doubled(): lax.ppermute(pieces, axis, [(i, i ^ distance) for i in range(devices)])]
    ppermute x0 -> x2, waiting for transfers between devices: none -> 1.61 us  [doubled(): lax.ppermute(pieces, axis, [(i, i ^ distance) for i in range(devices)])]
    unnamed x82 -> x53, local copies, waits for them, and re-layouts: 6.83 us -> 7.22 us
  transfers between devices with their start and end apart: 14 -> 16, of which waited for: 11 -> 12; matrix products, arithmetic and copies ran while one was open for 46% -> 50% of each run, Pallas kernels for 0% -> 0%
where the time goes in v1:
time: 100 us; the launch traced here: 98.8 us
  local copies, waits for them, and re-layouts  31.3 us (31%)
  starting transfers between devices  27.4 us (27%)
  other arithmetic  22.9 us (23%)
  waiting for transfers between devices  14.3 us (14%)
  blocking collectives  1.83 us (2%)
  between operations  1.17 us (1%)
    ppermute x7, starting transfers between devices, extended(): lax.ppermute(head, axis, [((i + 1) % count, i) for i in range(ends)])  11.8 us
    unnamed x35, other arithmetic  10.8 us
    ppermute x7, starting transfers between devices, extended(): lax.ppermute(tail, axis, [(i, (i + 1) % count) for i in range(ends)])  10.6 us
    ppermute x7, waiting for transfers between devices, extended(): lax.ppermute(tail, axis, [(i, (i + 1) % count) for i in range(ends)])  7.51 us
    unnamed x53, local copies, waits for them, and re-layouts  7.22 us
    slice x5, local copies, waits for them, and re-layouts, extended(): head = lax.slice_in_dim(cells, 0, width, axis=dim)  6.36 us
    ppermute x2, local copies, waits for them, and re-layouts, extended(): lax.ppermute(tail, axis, [(i, (i + 1) % count) for i in range(ends)])  6.09 us
    ppermute x7, waiting for transfers between devices, extended(): lax.ppermute(head, axis, [((i + 1) % count, i) for i in range(ends)])  5.19 us
  transfers between devices with their start and end apart: 16, of which 12 were waited for; matrix products, arithmetic and copies ran while one was open for 50% of the time, Pallas kernels for 0%

profile of v1, /device:TPU:0, one launch (start us, length us, event | category | flops | bytes accessed | tf_op | source)
XLA Modules:
  0.0 98.8 jit_solution(11388399996223807255)
XLA Ops:
  0.6 5.5 %collective-permute-start.14 = (f32[2,1,2,64]{3,2,1,0:T(2,128)}, f32[2,1,2,64]{3,2,1,0:T(2,128)}, u32[]{:S(2)}, u32[]{:S(2)}) collective-permute-start(f32[2,1,2,64]{3,2,1,0:T(2,128)} %param.56), channel_id=1, source_target_pairs={{0,8},{8,16},{16,24},{1,9},{9,17},{17,25},{2,10},{10,18},{18,26},{... | collective-permute-start | bytes 3080 | tf_op jit(solution)/shard_map/ppermute | solution.py:72
  6.2 1.3 %collective-permute-start.15 = (f32[2,1,2,64]{3,2,1,0:T(2,128)}, f32[2,1,2,64]{3,2,1,0:T(2,128)}, u32[]{:S(2)}, u32[]{:S(2)}) collective-permute-start(f32[2,1,2,64]{3,2,1,0:T(2,128)} %param.56), channel_id=1, source_target_pairs={{8,0},{16,8},{24,16},{9,1},{17,9},{25,17},{10,2},{18,10},{26,18},{... | collective-permute-start | bytes 3080 | tf_op jit(solution)/shard_map/ppermute | solution.py:74
  7.5 1.2 %constant_dynamic-update-slice_fusion.18 = (f32[19,8,8,128]{3,2,1,0:T(8,128)S(1)}, f32[8,8,128]{2,1,0:T(8,128)S(1)}, f32[8,8,128]{2,1,0:T(8,128)S(1)}, f32[8,8,1...) fusion(f32[19,8,8,128]{3,2,1,0:T(8,128)} %param.53, ...), kind=kLoop, calls=%fused_computation.20 | loop fusion | flops 589823 | bytes 860160
  8.6 0.8 constant_dynamic-update-slice_fusion.17
  9.4 0.8 constant_dynamic-update-slice_fusion.16
  10.3 0.8 constant_dynamic-update-slice_fusion.15
  11.8 2.7 %collective-permute-start = (f32[19,1,8,128]{3,2,1,0:T(8,128)S(1)}, f32[19,1,8,128]{3,2,1,0:T(8,128)S(1)}, u32[]{:S(2)}, u32[]{:S(2)}) collective-permute-start(f32[19,1,8,128]{3,2,1,0:T(8,128)S(1)} %get-tuple-element.383), channel_id=1, source_target_pairs={{0,8},{8,16},{16,24},{24,0},{1,9},{9,17},{17,25},{25,1},{2,10},{10... | collective-permute-start | bytes 233480 | tf_op jit(solution)/shard_map/ppermute | solution.py:72
  14.5 1.1 %collective-permute-start.1 = (f32[19,1,8,128]{3,2,1,0:T(8,128)S(1)}, f32[19,1,8,128]{3,2,1,0:T(8,128)S(1)}, u32[]{:S(2)}, u32[]{:S(2)}) collective-permute-start(f32[19,1,8,128]{3,2,1,0:T(8,128)S(1)} %get-tuple-element.384), channel_id=1, source_target_pairs={{8,0},{16,8},{24,16},{0,24},{9,1},{17,9},{25,17},{1,25},{10,2},{18... | collective-permute-start | bytes 233480 | tf_op jit(solution)/shard_map/ppermute | solution.py:74
  15.6 0.7 fusion.365
  16.2 2.4 %collective-permute-done = f32[19,1,8,128]{3,2,1,0:T(8,128)S(1)} collective-permute-done((f32[19,1,8,128]{3,2,1,0:T(8,128)S(1)}, f32[19,1,8,128]{3,2,1,0:T(8,128)S(1)}, u32[]{:S(2)}, u32[]{:S(2)}) %collective-permute-start) | collective-permute-done | bytes 77856 | tf_op jit(solution)/shard_map/ppermute | solution.py:72
  18.6 0.9 collective-permute-done.1
  20.3 0.7 fusion.396
  21.5 1.7 %fusion.392 = (f32[19,10,10,1]{3,2,1,0:T(8,128)}, f32[19,10,10,1]{3,2,1,0:T(8,128)S(1)}) fusion(f32[19,10,10,128]{3,2,1,0:T(8,128)S(1)} %pad_maximum_fusion), kind=kLoop, calls=%fused_computation.688 | loop fusion | bytes 30400 | tf_op jit(solution)/shard_map/slice | solution.py:68
  23.2 2.1 %copy.69 = f32[19,10,10,1]{0,3,2,1:T(1,128)S(1)} copy(f32[19,10,10,1]{3,2,1,0:T(8,128)} %get-tuple-element.355) | data formatting | bytes 15200 | tf_op jit(solution)/shard_map/slice | solution.py:68
  25.4 3.6 %collective-permute-start.5 = (f32[19,10,10,1]{0,3,2,1:T(1,128)S(1)}, f32[19,10,10,1]{0,3,2,1:T(1,128)S(1)}, u32[]{:S(2)}, u32[]{:S(2)}) collective-permute-start(f32[19,10,10,1]{0,3,2,1:T(1,128)S(1)} %copy.69), channel_id=1, source_target_pairs={{1,0},{2,1},{3,2},{0,3},{5,4},{6,5},{7,6},{4,7},{9,8},{10,9},{11,1... | collective-permute-start | bytes 22808 | tf_op jit(solution)/shard_map/ppermute | solution.py:74
  29.0 0.8 copy.67
  29.9 1.0 %collective-permute-done.5 = f32[19,10,10,1]{0,3,2,1:T(1,128)S(1)} collective-permute-done((f32[19,10,10,1]{0,3,2,1:T(1,128)S(1)}, f32[19,10,10,1]{0,3,2,1:T(1,128)S(1)}, u32[]{:S(2)}, u32[]{:S(2)}) %collective-permute-start.5) | collective-permute-done | bytes 7632 | tf_op jit(solution)/shard_map/ppermute | solution.py:74
  31.0 1.6 %copy.70 = f32[19,10,10,1]{3,2,1,0:T(8,128)S(1)} copy(f32[19,10,10,1]{0,3,2,1:T(1,128)S(1)} %collective-permute-done.5) | data formatting | bytes 15200 | tf_op jit(solution)/shard_map/ppermute | solution.py:74
  32.7 3.0 %collective-permute-done.4 = f32[19,10,10,1]{0,3,2,1:T(1,128)S(1)} collective-permute-done((f32[19,10,10,1]{0,3,2,1:T(1,128)S(1)}, f32[19,10,10,1]{0,3,2,1:T(1,128)S(1)}, u32[]{:S(2)}, u32[]{:S(2)}) %collective-permute-start.4) | collective-permute-done | bytes 7632 | tf_op jit(solution)/shard_map/ppermute | solution.py:72
  35.7 2.7 %copy.68 = f32[19,10,10,1]{3,2,1,0:T(8,128)} copy(f32[19,10,10,1]{0,3,2,1:T(1,128)S(1)} %collective-permute-done.4) | data formatting | bytes 15200 | tf_op jit(solution)/shard_map/ppermute | solution.py:72
  38.4 1.0 maximum_bitcast_fusion.13
  39.5 1.3 %copy-done = f32[19,10,10,1]{3,2,1,0:T(8,128)S(1)} copy-done((f32[19,10,10,1]{3,2,1,0:T(8,128)S(1)}, f32[19,10,10,1]{3,2,1,0:T(8,128)}, u32[]{:S(2)}) %copy-start) | copy-done | bytes 7624
  41.8 0.7 constant_dynamic-update-slice_fusion.36
  42.4 0.6 constant_dynamic-update-slice_fusion.35
  43.2 0.6 constant_dynamic-update-slice_fusion.30
  43.8 0.6 constant_dynamic-update-slice_fusion.29
  44.5 0.6 constant_dynamic-update-slice_fusion.28
  45.1 0.6 constant_dynamic-update-slice_fusion.27
  45.8 0.6 constant_dynamic-update-slice_fusion.26
  46.4 0.6 constant_dynamic-update-slice_fusion.25
  47.0 0.6 constant_dynamic-update-slice_fusion.24
  47.7 0.7 constant_dynamic-update-slice_fusion.23
  48.5 2.1 %collective-permute-start.6 = (f32[19,1,8,128]{3,2,1,0:T(8,128)S(1)}, f32[19,1,8,128]{3,2,1,0:T(8,128)S(1)}, u32[]{:S(2)}, u32[]{:S(2)}) collective-permute-start(f32[19,1,8,128]{3,2,1,0:T(8,128)S(1)} %get-tuple-element.382), channel_id=1, source_target_pairs={{0,8},{8,16},{16,24},{24,0},{1,9},{9,17},{17,25},{25,1},{2,10},{10... | collective-permute-start | bytes 233480 | tf_op jit(solution)/shard_map/ppermute | solution.py:72
  50.6 0.8 collective-permute-start.7
  51.5 0.7 fusion.397
  52.1 1.7 %collective-permute-done.6 = f32[19,1,8,128]{3,2,1,0:T(8,128)S(1)} collective-permute-done((f32[19,1,8,128]{3,2,1,0:T(8,128)S(1)}, f32[19,1,8,128]{3,2,1,0:T(8,128)S(1)}, u32[]{:S(2)}, u32[]{:S(2)}) %collective-permute-start.6) | collective-permute-done | bytes 77856 | tf_op jit(solution)/shard_map/ppermute | solution.py:72
  53.8 1.2 %collective-permute-done.7 = f32[19,1,8,128]{3,2,1,0:T(8,128)S(1)} collective-permute-done((f32[19,1,8,128]{3,2,1,0:T(8,128)S(1)}, f32[19,1,8,128]{3,2,1,0:T(8,128)S(1)}, u32[]{:S(2)}, u32[]{:S(2)}) %collective-permute-start.7) | collective-permute-done | bytes 77856 | tf_op jit(solution)/shard_map/ppermute | solution.py:74
  57.0 1.7 %fusion.391 = (f32[19,10,10,1]{3,2,1,0:T(8,128)S(1)}, f32[19,10,10,1]{3,2,1,0:T(8,128)}) fusion(f32[19,10,10,128]{3,2,1,0:T(8,128)S(1)} %pad_maximum_fusion.1), kind=kLoop, calls=%fused_computation.687 | loop fusion | bytes 30400 | tf_op jit(solution)/shard_map/slice | solution.py:68
  58.7 2.1 %copy.71 = f32[19,10,10,1]{0,3,2,1:T(1,128)S(1)} copy(f32[19,10,10,1]{3,2,1,0:T(8,128)} %get-tuple-element.354) | data formatting | bytes 15200 | tf_op jit(solution)/shard_map/slice | solution.py:69
  60.9 0.8 copy.73
  61.7 4.0 %collective-permute-start.11 = (f32[19,10,10,1]{0,3,2,1:T(1,128)S(1)}, f32[19,10,10,1]{0,3,2,1:T(1,128)}, u32[]{:S(2)}, u32[]{:S(2)}) collective-permute-start(f32[19,10,10,1]{0,3,2,1:T(1,128)S(1)} %copy.73), channel_id=1, source_target_pairs={{1,0},{2,1},{3,2},{0,3},{5,4},{6,5},{7,6},{4,7},{9,8},{10,9},{11,1... | collective-permute-start | bytes 22808 | tf_op jit(solution)/shard_map/ppermute | solution.py:74
  65.7 1.7 %collective-permute-done.11 = f32[19,10,10,1]{0,3,2,1:T(1,128)} collective-permute-done((f32[19,10,10,1]{0,3,2,1:T(1,128)S(1)}, f32[19,10,10,1]{0,3,2,1:T(1,128)}, u32[]{:S(2)}, u32[]{:S(2)}) %collective-permute-start.11) | collective-permute-done | bytes 7632 | tf_op jit(solution)/shard_map/ppermute | solution.py:74
  67.5 2.4 %copy.74 = f32[19,10,10,1]{3,2,1,0:T(8,128)S(1)} copy(f32[19,10,10,1]{0,3,2,1:T(1,128)} %collective-permute-done.11) | data formatting | bytes 15200 | tf_op jit(solution)/shard_map/ppermute | solution.py:74
  70.6 0.7 constant_dynamic-update-slice_fusion.64
  71.9 3.4 %copy.72 = f32[19,10,10,1]{3,2,1,0:T(8,128)} copy(f32[19,10,10,1]{0,3,2,1:T(1,128)} %collective-permute-done.10) | data formatting | bytes 15200 | tf_op jit(solution)/shard_map/ppermute | solution.py:72
  75.3 1.1 %maximum_bitcast_fusion.3 = (f32[8,8,128]{2,1,0:T(8,128)S(1)}, f32[8,8,128]{2,1,0:T(8,128)S(1)}, f32[8,8,128]{2,1,0:T(8,128)S(1)}) fusion(f32[19,10,10,1]{3,2,1,0:T(8,128)} %copy.72, f32[19,10,1,128]{3,2,1,0:T(1,128)S(1)} %collective-permute-done.9, f32[19,10,1,128]{3,2,1,0:T(1,128)S(1)} %collective-permute-done.8, ...), kind=kLoop, calls=%fused_computation.399 | loop fusion | flops 106496 | bytes 1078704 | tf_op jit(solution)/shard_map/squeeze | solution.py:195
  76.8 0.8 constant_dynamic-update-slice_fusion.57
  77.5 0.7 constant_dynamic-update-slice_fusion.61
  78.2 0.7 constant_dynamic-update-slice_fusion.59
  79.0 0.8 constant_dynamic-update-slice_fusion.60
  79.7 0.7 constant_dynamic-update-slice_fusion.63
  80.5 1.4 %select_reduce_fusion = (f32[128]{0:T(128)}, f32[128]{0:T(128)}, f32[128]{0:T(128)}, f32[1,8,8,128]{3,2,1,0:T(8,128)S(1)}, f32[1,8,8,128]{3,2,1,0:T(8,128)S(1)},...) fusion(f32[8,8,128]{2,1,0:T(8,128)S(1)} %get-tuple-element.278,, ...), kind=kLoop, calls=%fused_computation.509 | loop fusion | flops 573056 | bytes 1612128 | tf_op jit(solution)/shard_map/reduce_sum | solution.py:150
  81.9 0.7 reduce_sum.37
  82.6 0.7 reduce_sum.40
  83.5 0.7 reduce_sum.55
  84.4 1.8 %all_gather.3 = f32[3,1,2,16]{3,1,0,2:T(1,128)S(1)} all-gather(f32[3,1,1,16]{3,1,0,2:T(1,128)S(1)} %fusion.364), channel_id=1, replica_groups=mesh['gz'=4,'gy'=2,'gx'=4] {'gy'}, dimensions={2}, use_global_device_ids=true | all-gather | bytes 576 | tf_op jit(solution)/shard_map/all_gather | solution.py:207
  86.3 0.8 constant_dynamic-update-slice_fusion.53
  87.1 0.8 constant_dynamic-update-slice_fusion.52
  87.9 0.8 constant_dynamic-update-slice_fusion.51
  88.6 0.8 constant_dynamic-update-slice_fusion.50
  89.5 0.8 constant_dynamic-update-slice_fusion.41
  90.3 4.8 %collective-permute-start.13 = (f32[2,3,1,2,16]{4,0,3,2,1:T(2,128)S(1)}, f32[2,3,1,2,16]{4,0,3,2,1:T(2,128)S(1)}, u32[]{:S(2)}, u32[]{:S(2)}) collective-permute-start(f32[2,3,1,2,16]{4,0,3,2,1:T(2,128)S(1)} %pad_maximum_fusion.38), channel_id=1, source_target_pairs={{0,2},{1,3},{2,0},{3,1},{4,6},{5,7},{6,4},{7,5},{8,10},{9,11},{10,... | collective-permute-start | bytes 2312 | tf_op jit(solution)/shard_map/ppermute | solution.py:51
  95.1 1.6 %collective-permute-done.13 = f32[2,3,1,2,16]{4,0,3,2,1:T(2,128)S(1)} collective-permute-done((f32[2,3,1,2,16]{4,0,3,2,1:T(2,128)S(1)}, f32[2,3,1,2,16]{4,0,3,2,1:T(2,128)S(1)}, u32[]{:S(2)}, u32[]{:S(2)}) %collective-permute-start.13) | collective-permute-done | bytes 800 | tf_op jit(solution)/shard_map/ppermute | solution.py:51
  97.4 1.4 %multiply_subtract_fusion = f32[2,1,2,64]{3,2,1,0:T(2,128)} fusion(f32[2,1,2,64]{3,2,1,0:T(2,128)S(1)} %copy-done.8, f32[2,1,2,1]{3,2,1,0:T(2,128)} %get-tuple-element.403, f32[2,1,2,63]{3,2,1,0:T(2,128)} %get-tuple-element.405, f32[2,1,2,63]{3,2,1,0:T(2,128)} %get-tuple-element.404, f32[2,1,2,1]{3,2,1,0:T(2,128)} %get-tuple-element.402, ...), kind=kLoop, calls=%fused_computation.682 | loop fusion | flops 10496 | bytes 11810 | tf_op jit(solution)/shard_map/sub | solution.py:177
  (122 shorter events, 8.3 us)
Async XLA Ops:
  0.6 10.4 %copy-start.2 = (f32[19,8,8,128]{3,2,1,0:T(8,128)S(1)}, f32[19,8,8,128]{3,2,1,0:T(8,128)}, u32[]{:S(2)}) copy-start(f32[19,8,8,128]{3,2,1,0:T(8,128)} %param.53) | copy-start | bytes 1867780
  0.6 96.7 %collective-permute-start.14 = (f32[2,1,2,64]{3,2,1,0:T(2,128)}, f32[2,1,2,64]{3,2,1,0:T(2,128)}, u32[]{:S(2)}, u32[]{:S(2)}) collective-permute-start(f32[2,1,2,64]{3,2,1,0:T(2,128)} %param.56), channel_id=1, source_target_pairs={{0,8},{8,16},{16,24},{1,9},{9,17},{17,25},{2,10},{10,18},{18,26},{... | collective-permute-start | bytes 3080 | tf_op jit(solution)/shard_map/ppermute | solution.py:72
  6.2 91.2 %collective-permute-start.15 = (f32[2,1,2,64]{3,2,1,0:T(2,128)}, f32[2,1,2,64]{3,2,1,0:T(2,128)}, u32[]{:S(2)}, u32[]{:S(2)}) collective-permute-start(f32[2,1,2,64]{3,2,1,0:T(2,128)} %param.56), channel_id=1, source_target_pairs={{8,0},{16,8},{24,16},{9,1},{17,9},{25,17},{10,2},{18,10},{26,18},{... | collective-permute-start | bytes 3080 | tf_op jit(solution)/shard_map/ppermute | solution.py:74
  11.2 4.3 %copy-start.7 = (f32[2,1,2,64]{3,2,1,0:T(2,128)S(1)}, f32[2,1,2,64]{3,2,1,0:T(2,128)}, u32[]{:S(2)}) copy-start(f32[2,1,2,64]{3,2,1,0:T(2,128)} %param.56) | copy-start | bytes 3076
  11.3 4.3 %copy-start.14 = (f32[2,1,2,64]{3,2,1,0:T(2,128)S(1)}, f32[2,1,2,64]{3,2,1,0:T(2,128)}, u32[]{:S(2)}) copy-start(f32[2,1,2,64]{3,2,1,0:T(2,128)} %param.57) | copy-start | bytes 3076
  11.3 4.3 %copy-start.15 = (f32[2]{0:T(128)S(1)}, f32[2]{0:T(128)}, u32[]{:S(2)}) copy-start(f32[2]{0:T(128)} %constant.562.clone) | copy-start | bytes 28
  11.3 4.3 %copy-start.16 = (f32[2]{0:T(128)S(1)}, f32[2]{0:T(128)}, u32[]{:S(2)}) copy-start(f32[2]{0:T(128)} %constant.563.clone) | copy-start | bytes 28
  11.8 6.9 %collective-permute-start = (f32[19,1,8,128]{3,2,1,0:T(8,128)S(1)}, f32[19,1,8,128]{3,2,1,0:T(8,128)S(1)}, u32[]{:S(2)}, u32[]{:S(2)}) collective-permute-start(f32[19,1,8,128]{3,2,1,0:T(8,128)S(1)} %get-tuple-element.383), channel_id=1, source_target_pairs={{0,8},{8,16},{16,24},{24,0},{1,9},{9,17},{17,25},{25,1},{2,10},{10... | collective-permute-start | bytes 233480 | tf_op jit(solution)/shard_map/ppermute | solution.py:72
  14.5 5.1 %collective-permute-start.1 = (f32[19,1,8,128]{3,2,1,0:T(8,128)S(1)}, f32[19,1,8,128]{3,2,1,0:T(8,128)S(1)}, u32[]{:S(2)}, u32[]{:S(2)}) collective-permute-start(f32[19,1,8,128]{3,2,1,0:T(8,128)S(1)} %get-tuple-element.384), channel_id=1, source_target_pairs={{8,0},{16,8},{24,16},{0,24},{9,1},{17,9},{25,17},{1,25},{10,2},{18... | collective-permute-start | bytes 233480 | tf_op jit(solution)/shard_map/ppermute | solution.py:74
  19.7 1.4 %collective-permute-start.2 = (f32[19,10,1,128]{3,2,1,0:T(1,128)S(1)}, f32[19,10,1,128]{3,2,1,0:T(1,128)S(1)}, u32[]{:S(2)}, u32[]{:S(2)}) collective-permute-start(f32[19,10,1,128]{3,2,1,0:T(1,128)S(1)} %get-tuple-element.375), channel_id=1, source_target_pairs={{0,4},{4,0},{1,5},{5,1},{2,6},{6,2},{3,7},{7,3},{8,12},{12,8},{9,1... | collective-permute-start | bytes 291848 | tf_op jit(solution)/shard_map/ppermute | solution.py:72
  19.8 1.4 %collective-permute-start.3 = (f32[19,10,1,128]{3,2,1,0:T(1,128)S(1)}, f32[19,10,1,128]{3,2,1,0:T(1,128)S(1)}, u32[]{:S(2)}, u32[]{:S(2)}) collective-permute-start(f32[19,10,1,128]{3,2,1,0:T(1,128)S(1)} %get-tuple-element.376), channel_id=1, source_target_pairs={{4,0},{0,4},{5,1},{1,5},{6,2},{2,6},{7,3},{3,7},{12,8},{8,12},{13,... | collective-permute-start | bytes 291848 | tf_op jit(solution)/shard_map/ppermute | solution.py:74
  25.4 4.5 %copy-start.13 = (s32[2,8,128]{2,1,0:T(8,128)S(1)}, s32[2,8,128]{2,1,0:T(8,128)}, u32[]{:S(2)}) copy-start(s32[2,8,128]{2,1,0:T(8,128)} %param.55) | copy-start | bytes 24580
  25.4 5.6 %collective-permute-start.5 = (f32[19,10,10,1]{0,3,2,1:T(1,128)S(1)}, f32[19,10,10,1]{0,3,2,1:T(1,128)S(1)}, u32[]{:S(2)}, u32[]{:S(2)}) collective-permute-start(f32[19,10,10,1]{0,3,2,1:T(1,128)S(1)} %copy.69), channel_id=1, source_target_pairs={{1,0},{2,1},{3,2},{0,3},{5,4},{6,5},{7,6},{4,7},{9,8},{10,9},{11,1... | collective-permute-start | bytes 22808 | tf_op jit(solution)/shard_map/ppermute | solution.py:74
  29.8 5.9 %collective-permute-start.4 = (f32[19,10,10,1]{0,3,2,1:T(1,128)S(1)}, f32[19,10,10,1]{0,3,2,1:T(1,128)S(1)}, u32[]{:S(2)}, u32[]{:S(2)}) collective-permute-start(f32[19,10,10,1]{0,3,2,1:T(1,128)S(1)} %copy.67), channel_id=1, source_target_pairs={{0,1},{1,2},{2,3},{3,0},{4,5},{5,6},{6,7},{7,4},{8,9},{9,10},{10,1... | collective-permute-start | bytes 22808 | tf_op jit(solution)/shard_map/ppermute | solution.py:72
  29.9 11.0 %copy-start.9 = (pred[1,8,128]{2,1,0:T(8,128)(4,1)}, pred[1,8,128]{2,1,0:T(8,128)(4,1)S(1)}, u32[]{:S(2)}) copy-start(pred[1,8,128]{2,1,0:T(8,128)(4,1)S(1)} %get-tuple-element.317) | copy-start | bytes 3076
  39.4 1.4 %copy-start = (f32[19,10,10,1]{3,2,1,0:T(8,128)S(1)}, f32[19,10,10,1]{3,2,1,0:T(8,128)}, u32[]{:S(2)}) copy-start(f32[19,10,10,1]{3,2,1,0:T(8,128)} %copy.68) | copy-start | bytes 22804
  40.9 0.6 copy-start.11
  48.5 5.3 %collective-permute-start.6 = (f32[19,1,8,128]{3,2,1,0:T(8,128)S(1)}, f32[19,1,8,128]{3,2,1,0:T(8,128)S(1)}, u32[]{:S(2)}, u32[]{:S(2)}) collective-permute-start(f32[19,1,8,128]{3,2,1,0:T(8,128)S(1)} %get-tuple-element.382), channel_id=1, source_target_pairs={{0,8},{8,16},{16,24},{24,0},{1,9},{9,17},{17,25},{25,1},{2,10},{10... | collective-permute-start | bytes 233480 | tf_op jit(solution)/shard_map/ppermute | solution.py:72
  50.6 4.4 %collective-permute-start.7 = (f32[19,1,8,128]{3,2,1,0:T(8,128)S(1)}, f32[19,1,8,128]{3,2,1,0:T(8,128)S(1)}, u32[]{:S(2)}, u32[]{:S(2)}) collective-permute-start(f32[19,1,8,128]{3,2,1,0:T(8,128)S(1)} %get-tuple-element.381), channel_id=1, source_target_pairs={{8,0},{16,8},{24,16},{0,24},{9,1},{17,9},{25,17},{1,25},{10,2},{18... | collective-permute-start | bytes 233480 | tf_op jit(solution)/shard_map/ppermute | solution.py:74
  55.2 1.4 %collective-permute-start.8 = (f32[19,10,1,128]{3,2,1,0:T(1,128)S(1)}, f32[19,10,1,128]{3,2,1,0:T(1,128)S(1)}, u32[]{:S(2)}, u32[]{:S(2)}) collective-permute-start(f32[19,10,1,128]{3,2,1,0:T(1,128)S(1)} %get-tuple-element.371), channel_id=1, source_target_pairs={{0,4},{4,0},{1,5},{5,1},{2,6},{6,2},{3,7},{7,3},{8,12},{12,8},{9,1... | collective-permute-start | bytes 291848 | tf_op jit(solution)/shard_map/ppermute | solution.py:72
  55.2 1.4 %collective-permute-start.9 = (f32[19,10,1,128]{3,2,1,0:T(1,128)S(1)}, f32[19,10,1,128]{3,2,1,0:T(1,128)S(1)}, u32[]{:S(2)}, u32[]{:S(2)}) collective-permute-start(f32[19,10,1,128]{3,2,1,0:T(1,128)S(1)} %get-tuple-element.372), channel_id=1, source_target_pairs={{4,0},{0,4},{5,1},{1,5},{6,2},{2,6},{7,3},{3,7},{12,8},{8,12},{13,... | collective-permute-start | bytes 291848 | tf_op jit(solution)/shard_map/ppermute | solution.py:74
  60.8 10.4 %collective-permute-start.10 = (f32[19,10,10,1]{0,3,2,1:T(1,128)S(1)}, f32[19,10,10,1]{0,3,2,1:T(1,128)}, u32[]{:S(2)}, u32[]{:S(2)}) collective-permute-start(f32[19,10,10,1]{0,3,2,1:T(1,128)S(1)} %copy.71), channel_id=1, source_target_pairs={{0,1},{1,2},{2,3},{3,0},{4,5},{5,6},{6,7},{7,4},{8,9},{9,10},{10,1... | collective-permute-start | bytes 22808 | tf_op jit(solution)/shard_map/ppermute | solution.py:72
  61.7 5.8 %collective-permute-start.11 = (f32[19,10,10,1]{0,3,2,1:T(1,128)S(1)}, f32[19,10,10,1]{0,3,2,1:T(1,128)}, u32[]{:S(2)}, u32[]{:S(2)}) collective-permute-start(f32[19,10,10,1]{0,3,2,1:T(1,128)S(1)} %copy.73), channel_id=1, source_target_pairs={{1,0},{2,1},{3,2},{0,3},{5,4},{6,5},{7,6},{4,7},{9,8},{10,9},{11,1... | collective-permute-start | bytes 22808 | tf_op jit(solution)/shard_map/ppermute | solution.py:74
  69.9 0.7 copy-start.12
  71.3 0.6 copy-start.4
  75.3 1.5 %copy-start.1 = (f32[19,10,10,1]{3,2,1,0:T(8,128)S(1)}, f32[19,10,10,1]{3,2,1,0:T(8,128)}, u32[]{:S(2)}) copy-start(f32[19,10,10,1]{3,2,1,0:T(8,128)} %copy.72) | copy-start | bytes 22804
  75.3 1.5 %copy-start.10 = (pred[1,8,128]{2,1,0:T(8,128)(4,1)S(1)}, pred[1,8,128]{2,1,0:T(8,128)(4,1)}, u32[]{:S(2)}) copy-start(pred[1,8,128]{2,1,0:T(8,128)(4,1)} %copy-done.9) | copy-start | bytes 3076
  79.0 1.5 %copy-start.5 = (f32[8,8,128]{2,1,0:T(8,128)S(1)}, f32[8,8,128]{2,1,0:T(8,128)}, u32[]{:S(2)}) copy-start(f32[8,8,128]{2,1,0:T(8,128)} %copy-done.4) | copy-start | bytes 98308
  79.0 1.5 %copy-start.6 = (s32[8,8,128]{2,1,0:T(8,128)S(1)}, s32[8,8,128]{2,1,0:T(8,128)}, u32[]{:S(2)}) copy-start(s32[8,8,128]{2,1,0:T(8,128)} %param.54) | copy-start | bytes 98308
  80.5 16.9 %copy-start.8 = (f32[2,1,2,64]{3,2,1,0:T(2,128)S(1)}, f32[2,1,2,64]{3,2,1,0:T(2,128)}, u32[]{:S(2)}) copy-start(f32[2,1,2,64]{3,2,1,0:T(2,128)} %param.56) | copy-start | bytes 3076
  86.2 4.0 %collective-permute-start.12 = (f32[1,3,1,2,16]{4,0,3,2,1:T(1,128)S(1)}, f32[1,3,1,2,16]{4,0,3,2,1:T(1,128)S(1)}, u32[]{:S(2)}, u32[]{:S(2)}) collective-permute-start(f32[1,3,1,2,16]{4,0,3,2,1:T(1,128)S(1)} %bitcast.625), channel_id=1, source_target_pairs={{0,1},{1,0},{2,3},{3,2},{4,5},{5,4},{6,7},{7,6},{8,9},{9,8},{10,11... | collective-permute-start | bytes 1160 | tf_op jit(solution)/shard_map/ppermute | solution.py:51
  90.3 6.4 %collective-permute-start.13 = (f32[2,3,1,2,16]{4,0,3,2,1:T(2,128)S(1)}, f32[2,3,1,2,16]{4,0,3,2,1:T(2,128)S(1)}, u32[]{:S(2)}, u32[]{:S(2)}) collective-permute-start(f32[2,3,1,2,16]{4,0,3,2,1:T(2,128)S(1)} %pad_maximum_fusion.38), channel_id=1, source_target_pairs={{0,2},{1,3},{2,0},{3,1},{4,6},{5,7},{6,4},{7,5},{8,10},{9,11},{10,... | collective-permute-start | bytes 2312 | tf_op jit(solution)/shard_map/ppermute | solution.py:51
  95.1 3.7 %copy-start.3 = (f32[19,8,8,128]{3,2,1,0:T(8,128)}, f32[19,8,8,128]{3,2,1,0:T(8,128)S(1)}, u32[]{:S(2)}) copy-start(f32[19,8,8,128]{3,2,1,0:T(8,128)S(1)} %constant_dynamic-update-slice_fusion.38) | copy-start | bytes 1867780
